TPU v7x, 32 devices: a whole 2x2x4 slice. The times are simulated.
32 devices in a mesh: dp: 4 (over x, core), tensor: 8 (over z, y).
Axes of the slice: x: 2, y: 2, z: 4, core: 2. Of those that a mesh axis runs over, the one named last changes fastest.
Arguments:
- tokens: bfloat16 [2, 2048, 4, 1024], P(None, 'tensor', 'dp'), may hold values from -6 to 6
- cotangent: bfloat16 [2, 2048, 4, 1024], P(None, 'tensor', 'dp'), may hold values from -6 to 6
- timesteps: int32 [2, 4, 2], P(None, 'dp'), may hold values from 0 to 999
- bucket: int32 [2, 4], P(None, 'dp'), may hold values 0 or 1
- counts: int32 [2, 4], P(None, 'dp'), may hold values from 8 to 48, as said below
- qkv_weight: bfloat16 [3, 1024, 1024], P(None, None, 'tensor'), may hold values from -0.1875 to 0.1875
- qv_bias: float32 [2, 1024], P(None, 'tensor'), may hold values from -3 to 3
- out_weight: bfloat16 [1024, 1024], P('tensor'), may hold values from -2 to 2
- out_bias: float32 [1024], replicated, may hold values from -2 to 2
- norm1_gain: float32 [1024], replicated, may hold values from 0.25 to 1.75
- norm1_bias: float32 [1024], replicated, may hold values from -2 to 2
- up_weight: bfloat16 [1024, 4096], P(None, 'tensor'), may hold values from -0.1875 to 0.1875
- up_bias: float32 [4096], P('tensor'), may hold values from -3 to 3
- down_weight: bfloat16 [4096, 1024], P('tensor'), may hold values from -0.09375 to 0.09375
- down_bias: float32 [1024], replicated, may hold values from -2 to 2
- norm2_gain: float32 [1024], replicated, may hold values from 0.25 to 1.75
- norm2_bias: float32 [1024], replicated, may hold values from -2 to 2
Outputs:
- layer_out: bfloat16 [2, 2048, 4, 1024], P(None, 'tensor', 'dp')
- tokens_grad: float32 [2, 2048, 4, 1024], P(None, 'tensor', 'dp')
- qkv_grad: float32 [3, 1024, 1024], P(None, 'dp', 'tensor')
- qv_bias_grad: float32 [2, 1024], P(None, ('tensor', 'dp'))
- out_weight_grad: float32 [1024, 1024], P('tensor', 'dp')
- up_weight_grad: float32 [1024, 4096], P('dp', 'tensor')
- up_bias_grad: float32 [4096], P(('tensor', 'dp'))
- down_weight_grad: float32 [4096, 1024], P('tensor', 'dp')
- vector_grads: float32 [6, 1024], P(None, ('dp', 'tensor'))
Inputs may be any that keep to these rules, and one draw needn't show every extreme that they name: True counts are positive.
All inputs are finite; a program needn't handle non-finite values. No bound on the sum of `bucket` on one device may be relied on, other than what follows from the above.
Results may differ from a plain program's by a relative error of at most 0.02.
Values may be sent and summed in bfloat16 or wider, within the bound.
A program may use at most 320 MiB of HBM per device.

v0:
```python
import math
import jax
import jax.numpy as jnp
from jax import lax
from jax.sharding import PartitionSpec as P

HD = 64
EPS = 1e-05
INV_ROOT_TWO = 1.0 / math.sqrt(2.0)
INV_ROOT_TWO_PI = 1.0 / math.sqrt(2.0 * math.pi)


def as_sent(array):

    def short(part):
        return part.astype(jnp.bfloat16) if part.dtype == jnp.float32 else part

    return jax.tree.map(short, array)


def sinusoid(steps, width):
    half_width = width // 2
    freqs = jnp.exp(jnp.arange(half_width).astype(jnp.float32) * (-2.0 * math.log(10000.0) / width))
    angles = steps.astype(jnp.float32)[..., None] * freqs
    return jnp.concatenate([jnp.sin(angles), jnp.cos(angles)], axis=-1)


def norm_forward(values, gain, shift):
    average = jnp.mean(values, axis=-1, keepdims=True)
    centred = values - average
    spread = jnp.mean(centred * centred, axis=-1, keepdims=True)
    inverse = lax.rsqrt(spread + EPS)
    unit = centred * inverse
    return (unit * gain + shift, unit, inverse)


def norm_backward(grad, unit, inverse, gain):
    scaled = grad * gain
    first = jnp.mean(scaled, axis=-1, keepdims=True)
    second = jnp.mean(scaled * unit, axis=-1, keepdims=True)
    return inverse * (scaled - first - unit * second)


def gelu_slope(pre):
    return (
        0.5 * (1.0 + lax.erf(pre * INV_ROOT_TWO))
        + pre * jnp.exp(-0.5 * pre * pre) * INV_ROOT_TWO_PI
    )


def add_trees(left, right):
    if left is None:
        return right
    return jax.tree.map(lambda first_one, second_one: first_one + second_one, left, right)


def body(
    tokens,
    cotangent,
    timesteps,
    bucket,
    counts,
    qkv_weight,
    qv_bias,
    out_weight,
    out_bias,
    norm1_gain,
    norm1_bias,
    up_weight,
    up_bias,
    down_weight,
    down_bias,
    norm2_gain,
    norm2_bias,
):
    micro, segment, items_loc, width = tokens.shape
    parts = lax.axis_size("tensor")
    seq_len = segment * parts
    half_len = seq_len // 2
    columns = qkv_weight.shape[2]
    heads_loc = columns // HD
    scale = float(HD) ** (-0.5)
    position = lax.axis_index("tensor") * segment + jnp.arange(segment)
    late = position >= half_len
    count_f = counts.astype(jnp.float32)
    total = lax.psum(jnp.sum(count_f), "dp")
    items_all = micro * items_loc * lax.axis_size("dp")
    item_weight = count_f * float(items_all) / total
    outputs = []
    input_grads = []
    totals = None
    vector_total = jnp.zeros((6, width), jnp.float32)
    for index in range(micro):
        embedded = sinusoid(timesteps[index], width)
        temb = jnp.where(late[:, None, None], embedded[None, :, 1], embedded[None, :, 0])
        hidden = tokens[index].astype(jnp.float32) + temb
        hidden_low = hidden.astype(jnp.bfloat16)
        hidden_all = lax.all_gather(hidden_low, "tensor", axis=0, tiled=True)
        projected = jnp.einsum(
            "sid,kdc->ksic", hidden_all, qkv_weight, preferred_element_type=jnp.float32
        )
        q_heads = (
            (projected[0] + qv_bias[0])
            .astype(jnp.bfloat16)
            .reshape(seq_len, items_loc, heads_loc, HD)
        )
        k_heads = projected[1].astype(jnp.bfloat16).reshape(seq_len, items_loc, heads_loc, HD)
        v_heads = (
            (projected[2] + qv_bias[1])
            .astype(jnp.bfloat16)
            .reshape(seq_len, items_loc, heads_loc, HD)
        )
        logsums = []
        pieces = []
        for block in range(2):
            limit = (block + 1) * half_len
            scores = (
                jnp.einsum(
                    "qihd,kihd->ihqk",
                    q_heads[block * half_len : limit],
                    k_heads[:limit],
                    preferred_element_type=jnp.float32,
                )
                * scale
            )
            highest = jnp.max(scores, axis=-1, keepdims=True)
            logsum = highest + jnp.log(jnp.sum(jnp.exp(scores - highest), axis=-1, keepdims=True))
            probs_low = jnp.exp(scores - logsum).astype(jnp.bfloat16)
            pieces.append(
                jnp.einsum(
                    "ihqk,kihd->qihd",
                    probs_low,
                    v_heads[:limit],
                    preferred_element_type=jnp.float32,
                )
            )
            logsums.append(logsum)
        context = (
            jnp.concatenate(pieces, axis=0)
            .reshape(seq_len, items_loc, columns)
            .astype(jnp.bfloat16)
        )
        attention = lax.psum_scatter(
            jnp.einsum(
                "sic,cd->sid", context, out_weight, preferred_element_type=jnp.float32
            ).astype(jnp.bfloat16),
            "tensor",
            scatter_dimension=0,
            tiled=True,
        ).astype(jnp.float32)
        normed, unit_one, inverse_one = norm_forward(
            hidden + (attention + out_bias), norm1_gain, norm1_bias
        )
        normed_low = normed.astype(jnp.bfloat16)
        normed_all = lax.all_gather(normed_low, "tensor", axis=0, tiled=True)
        pre = (
            jnp.einsum("sid,df->sif", normed_all, up_weight, preferred_element_type=jnp.float32)
            + up_bias
        )
        act_low = jax.nn.gelu(pre, approximate=False).astype(jnp.bfloat16)
        branch = lax.psum_scatter(
            jnp.einsum(
                "sif,fd->sid", act_low, down_weight, preferred_element_type=jnp.float32
            ).astype(jnp.bfloat16),
            "tensor",
            scatter_dimension=0,
            tiled=True,
        ).astype(jnp.float32)
        result, unit_two, inverse_two = norm_forward(
            normed + (branch + down_bias), norm2_gain, norm2_bias
        )
        outputs.append(result.astype(jnp.bfloat16))
        keep = jnp.where(late[:, None], bucket[index][None, :], 1).astype(jnp.float32)
        grad_out = (
            cotangent[index].astype(jnp.float32)
            * item_weight[index][None, :, None]
            * keep[:, :, None]
        )
        gain_two_grad = jnp.sum(grad_out * unit_two, axis=(0, 1))
        shift_two_grad = jnp.sum(grad_out, axis=(0, 1))
        grad_sum = norm_backward(grad_out, unit_two, inverse_two, norm2_gain)
        down_bias_grad = jnp.sum(grad_sum, axis=(0, 1))
        grad_sum_all = lax.all_gather(grad_sum.astype(jnp.bfloat16), "tensor", axis=0, tiled=True)
        grad_act = jnp.einsum(
            "sid,fd->sif", grad_sum_all, down_weight, preferred_element_type=jnp.float32
        )
        down_grad = jnp.einsum(
            "sif,sid->fd", act_low, grad_sum_all, preferred_element_type=jnp.float32
        )
        grad_pre = (grad_act * gelu_slope(pre)).astype(jnp.bfloat16)
        up_bias_part = jnp.sum(grad_pre, axis=(0, 1), dtype=jnp.float32)
        up_grad = jnp.einsum(
            "sid,sif->df", normed_all, grad_pre, preferred_element_type=jnp.float32
        )
        grad_through = lax.psum_scatter(
            jnp.einsum(
                "sif,df->sid", grad_pre, up_weight, preferred_element_type=jnp.float32
            ).astype(jnp.bfloat16),
            "tensor",
            scatter_dimension=0,
            tiled=True,
        ).astype(jnp.float32)
        grad_normed = grad_sum + grad_through
        gain_one_grad = jnp.sum(grad_normed * unit_one, axis=(0, 1))
        shift_one_grad = jnp.sum(grad_normed, axis=(0, 1))
        grad_mixed = norm_backward(grad_normed, unit_one, inverse_one, norm1_gain)
        out_bias_grad = jnp.sum(grad_mixed, axis=(0, 1))
        grad_mixed_all = lax.all_gather(
            grad_mixed.astype(jnp.bfloat16), "tensor", axis=0, tiled=True
        )
        grad_context = jnp.einsum(
            "sid,cd->sic", grad_mixed_all, out_weight, preferred_element_type=jnp.float32
        ).astype(jnp.bfloat16)
        out_grad = jnp.einsum(
            "sic,sid->cd", context, grad_mixed_all, preferred_element_type=jnp.float32
        )
        grad_ctx_heads = grad_context.reshape(seq_len, items_loc, heads_loc, HD)
        query_grads = []
        key_total = jnp.zeros((seq_len, items_loc, heads_loc, HD), jnp.float32)
        value_total = jnp.zeros((seq_len, items_loc, heads_loc, HD), jnp.float32)
        for block in range(2):
            limit = (block + 1) * half_len
            rows_q = q_heads[block * half_len : limit]
            rows_grad = grad_ctx_heads[block * half_len : limit]
            scores = (
                jnp.einsum(
                    "qihd,kihd->ihqk", rows_q, k_heads[:limit], preferred_element_type=jnp.float32
                )
                * scale
            )
            probs = jnp.exp(scores - logsums[block])
            probs_low = probs.astype(jnp.bfloat16)
            grad_probs = jnp.einsum(
                "qihd,kihd->ihqk", rows_grad, v_heads[:limit], preferred_element_type=jnp.float32
            )
            value_part = jnp.einsum(
                "ihqk,qihd->kihd", probs_low, rows_grad, preferred_element_type=jnp.float32
            )
            grad_scores = (
                probs * (grad_probs - jnp.sum(probs * grad_probs, axis=-1, keepdims=True))
            ).astype(jnp.bfloat16)
            query_grads.append(
                jnp.einsum(
                    "ihqk,kihd->qihd",
                    grad_scores,
                    k_heads[:limit],
                    preferred_element_type=jnp.float32,
                )
                * scale
            )
            key_part = (
                jnp.einsum(
                    "ihqk,qihd->kihd", grad_scores, rows_q, preferred_element_type=jnp.float32
                )
                * scale
            )
            padding = ((0, seq_len - limit), (0, 0), (0, 0), (0, 0))
            key_total = key_total + jnp.pad(key_part, padding)
            value_total = value_total + jnp.pad(value_part, padding)
        grad_queries = (
            jnp.concatenate(query_grads, axis=0)
            .reshape(seq_len, items_loc, columns)
            .astype(jnp.bfloat16)
        )
        grad_keys = key_total.reshape(seq_len, items_loc, columns).astype(jnp.bfloat16)
        grad_values = value_total.reshape(seq_len, items_loc, columns).astype(jnp.bfloat16)
        grad_stack = jnp.stack([grad_queries, grad_keys, grad_values])
        bias_grad = jnp.stack(
            [
                jnp.sum(grad_queries, axis=(0, 1), dtype=jnp.float32),
                jnp.sum(grad_values, axis=(0, 1), dtype=jnp.float32),
            ]
        )
        qkv_part = jnp.einsum(
            "sid,ksic->kdc", hidden_all, grad_stack, preferred_element_type=jnp.float32
        )
        grad_proj = lax.psum_scatter(
            jnp.einsum(
                "ksic,kdc->sid", grad_stack, qkv_weight, preferred_element_type=jnp.float32
            ).astype(jnp.bfloat16),
            "tensor",
            scatter_dimension=0,
            tiled=True,
        ).astype(jnp.float32)
        grad_hidden = grad_mixed + grad_proj
        input_grads.append(grad_hidden)
        vector_total = vector_total + jnp.stack(
            [
                out_bias_grad,
                gain_one_grad,
                shift_one_grad,
                down_bias_grad,
                gain_two_grad,
                shift_two_grad,
            ]
        )
        micro_grads = (qkv_part, bias_grad, up_grad[None], up_bias_part[None], out_grad, down_grad)
        totals = add_trees(totals, micro_grads)
    totals = jax.tree.map(
        lambda part: part.astype(jnp.float32),
        lax.psum_scatter(as_sent(totals), "dp", scatter_dimension=1, tiled=True),
    )
    vector_grads = lax.psum_scatter(vector_total, ("dp", "tensor"), scatter_dimension=1, tiled=True)
    layer_out = jnp.stack(outputs)
    tokens_grad = jnp.stack(input_grads)
    return (
        layer_out,
        tokens_grad,
        totals[0],
        totals[1],
        totals[4],
        totals[2][0],
        totals[3][0],
        totals[5],
        vector_grads,
    )


def solution(mesh):
    placed = (
        P(None, "tensor", "dp", None),
        P(None, "tensor", "dp", None),
        P(None, "dp", None),
        P(None, "dp"),
        P(None, "dp"),
        P(None, None, "tensor"),
        P(None, "tensor"),
        P("tensor", None),
        P(),
        P(),
        P(),
        P(None, "tensor"),
        P("tensor"),
        P("tensor", None),
        P(),
        P(),
        P(),
    )
    return jax.shard_map(
        body,
        mesh=mesh,
        in_specs=placed,
        out_specs=(
            P(None, "tensor", "dp", None),
            P(None, "tensor", "dp", None),
            P(None, "dp", "tensor"),
            P(None, ("tensor", "dp")),
            P("tensor", "dp"),
            P("dp", "tensor"),
            P(("tensor", "dp")),
            P("tensor", "dp"),
            P(None, ("dp", "tensor")),
        ),
        check_vma=False,
    )
```

profile of v0, /device:TPU:0, one launch (start us, length us, event | category | flops | bytes accessed | tf_op | source)
XLA Modules:
  0.0 1731.8 jit_solution(11281601683911485581)
XLA Ops:
  13.5 72.8 %all-gather.9.cloned.1.call-done = bf16[2048,1,1024]{2,0,1:T(8,128)(2,1)} async-done(((bf16[256,1,1024]{2,0,1:T(8,128)(2,1)}), bf16[2048,1,1024]{2,0,1:T(8,128)(2,1)}) %all-gather.9.cloned.1.call-update) | async-done | bytes 4194320 | tf_op jit(solution)/shard_map/all_gather | solution.py:98
  111.0 86.9 %reduce-scatter.22.cloned.1.call-done = bf16[256,1,1024]{2,0,1:T(8,128)(2,1)} async-done(((bf16[2048,1,1024]{2,0,1:T(8,128)(2,1)}), bf16[256,1,1024]{2,0,1:T(8,128)(2,1)}) %reduce-scatter.22.cloned.1.call-update) | async-done | bytes 524304 | tf_op jit(solution)/shard_map/reduce_scatter | solution.py:143
  201.3 72.0 %all-gather.13.cloned.1.call-done = bf16[2048,1,1024]{2,0,1:T(8,128)(2,1)} async-done(((bf16[256,1,1024]{2,0,1:T(8,128)(2,1)}), bf16[2048,1,1024]{2,0,1:T(8,128)(2,1)}) %all-gather.13.cloned.1.call-update) | async-done | bytes 4194320 | tf_op jit(solution)/shard_map/all_gather | solution.py:98
  299.1 86.9 %reduce-scatter.26.cloned.1.call-done = bf16[256,1,1024]{2,0,1:T(8,128)(2,1)} async-done(((bf16[2048,1,1024]{2,0,1:T(8,128)(2,1)}), bf16[256,1,1024]{2,0,1:T(8,128)(2,1)}) %reduce-scatter.26.cloned.1.call-update) | async-done | bytes 524304 | tf_op jit(solution)/shard_map/reduce_scatter | solution.py:143
  389.1 72.5 %all-gather.11.cloned.1.call-done = bf16[2048,1,1024]{2,0,1:T(8,128)(2,1)} async-done(((bf16[256,1,1024]{2,0,1:T(8,128)(2,1)}), bf16[2048,1,1024]{2,0,1:T(8,128)(2,1)}) %all-gather.11.cloned.1.call-update) | async-done | bytes 4194320 | tf_op jit(solution)/shard_map/all_gather | solution.py:155
  461.7 14.0 fusion.6
  491.4 77.0 %reduce-scatter.24.cloned.1.call-done = bf16[256,1,1024]{2,0,1:T(8,128)(2,1)} async-done(((bf16[2048,1,1024]{2,0,1:T(8,128)(2,1)}), bf16[256,1,1024]{2,0,1:T(8,128)(2,1)}) %reduce-scatter.24.cloned.1.call-update) | async-done | bytes 524304 | tf_op jit(solution)/shard_map/reduce_scatter | solution.py:161
  576.4 72.5 %all-gather.17.cloned.1.call-done = bf16[2048,1,1024]{2,0,1:T(8,128)(2,1)} async-done(((bf16[256,1,1024]{2,0,1:T(8,128)(2,1)}), bf16[2048,1,1024]{2,0,1:T(8,128)(2,1)}) %all-gather.17.cloned.1.call-update) | async-done | bytes 4194320 | tf_op jit(solution)/shard_map/all_gather | solution.py:183
  662.1 86.5 %reduce-scatter.30.cloned.1.call-done = bf16[256,1,1024]{2,0,1:T(8,128)(2,1)} async-done(((bf16[2048,1,1024]{2,0,1:T(8,128)(2,1)}), bf16[256,1,1024]{2,0,1:T(8,128)(2,1)}) %reduce-scatter.30.cloned.1.call-update) | async-done | bytes 524304 | tf_op jit(solution)/shard_map/reduce_scatter | solution.py:195
  753.1 72.5 %all-gather.15.cloned.1.call-done = bf16[2048,1,1024]{2,0,1:T(8,128)(2,1)} async-done(((bf16[256,1,1024]{2,0,1:T(8,128)(2,1)}), bf16[2048,1,1024]{2,0,1:T(8,128)(2,1)}) %all-gather.15.cloned.1.call-update) | async-done | bytes 4194320 | tf_op jit(solution)/shard_map/all_gather | solution.py:155
  825.7 13.9 fusion.9
  845.9 86.3 %reduce-scatter.28.cloned.1.call-done = bf16[256,1,1024]{2,0,1:T(8,128)(2,1)} async-done(((bf16[2048,1,1024]{2,0,1:T(8,128)(2,1)}), bf16[256,1,1024]{2,0,1:T(8,128)(2,1)}) %reduce-scatter.28.cloned.1.call-update) | async-done | bytes 524304 | tf_op jit(solution)/shard_map/reduce_scatter | solution.py:161
  944.5 67.8 %all-gather.21.cloned.1.call-done = bf16[2048,1,1024]{2,0,1:T(8,128)(2,1)} async-done(((bf16[256,1,1024]{2,0,1:T(8,128)(2,1)}), bf16[2048,1,1024]{2,0,1:T(8,128)(2,1)}) %all-gather.21.cloned.1.call-update) | async-done | bytes 4194320 | tf_op jit(solution)/shard_map/all_gather | solution.py:183
  1025.2 60.4 %all-gather.19.cloned.1.call-done = bf16[2048,1,1024]{2,0,1:T(8,128)(2,1)} async-done(((bf16[256,1,1024]{2,0,1:T(8,128)(2,1)}), bf16[2048,1,1024]{2,0,1:T(8,128)(2,1)}) %all-gather.19.cloned.1.call-update) | async-done | bytes 4194320 | tf_op jit(solution)/shard_map/all_gather | solution.py:208
  1096.6 79.5 %reduce-scatter.34.cloned.1.call-done = bf16[256,1,1024]{2,0,1:T(8,128)(2,1)} async-done(((bf16[2048,1,1024]{2,0,1:T(8,128)(2,1)}), bf16[256,1,1024]{2,0,1:T(8,128)(2,1)}) %reduce-scatter.34.cloned.1.call-update) | async-done | bytes 524304 | tf_op jit(solution)/shard_map/reduce_scatter | solution.py:195
  1192.5 14.9 multiply_reduce_fusion.1
  1347.8 20.1 %reduce-scatter.48.cloned.1.call-done = bf16[128,1]{1,0:T(8,128)(2,1)} async-done(((bf16[512,1]{1,0:T(8,128)(2,1)}), bf16[128,1]{1,0:T(8,128)(2,1)}) %reduce-scatter.48.cloned.1.call-update) | async-done | bytes 272
  1369.3 25.8 %reduce-scatter.44.cloned.1.call-done = bf16[512,256]{1,0:T(8,128)(2,1)} async-done(((bf16[512,1024]{1,0:T(8,128)(2,1)}), bf16[512,256]{1,0:T(8,128)(2,1)}) %reduce-scatter.44.cloned.1.call-update) | async-done | bytes 262160 | tf_op jit(solution)/shard_map/reduce_scatter | solution.py:301
  1396.9 26.0 %reduce-scatter.42.cloned.1.call-done = bf16[1,256,512]{2,1,0:T(8,128)(2,1)} async-done(((bf16[1,1024,512]{2,1,0:T(8,128)(2,1)}), bf16[1,256,512]{2,1,0:T(8,128)(2,1)}) %reduce-scatter.42.cloned.1.call-update) | async-done | bytes 262160 | tf_op jit(solution)/shard_map/reduce_scatter | solution.py:301
  1424.7 136.4 %reduce-scatter.50.cloned.1.call-done = f32[32,6]{1,0:T(8,128)} async-done(((f32[1024,6]{1,0:T(8,128)}), f32[32,6]{1,0:T(8,128)}) %reduce-scatter.50.cloned.1.call-update) | async-done | bytes 784
  1562.4 16.8 reduce-scatter.46.cloned.1.call-done
  1580.5 21.8 %reduce-scatter.40.cloned.1.call-done = bf16[128,256]{1,0:T(8,128)(2,1)} async-done(((bf16[128,1024]{1,0:T(8,128)(2,1)}), bf16[128,256]{1,0:T(8,128)(2,1)}) %reduce-scatter.40.cloned.1.call-update) | async-done | bytes 65552 | tf_op jit(solution)/shard_map/reduce_scatter | solution.py:301
  1603.8 24.3 %reduce-scatter.38.cloned.1.call-done = bf16[3,256,128]{1,2,0:T(8,128)(2,1)} async-done(((bf16[3,1024,128]{1,2,0:T(8,128)(2,1)}), bf16[3,256,128]{1,2,0:T(8,128)(2,1)}) %reduce-scatter.38.cloned.1.call-update) | async-done | bytes 196624 | tf_op jit(solution)/shard_map/reduce_scatter | solution.py:301
  1629.9 90.2 %reduce-scatter.36.cloned.1.call-done = bf16[256,1,1024]{2,0,1:T(8,128)(2,1)} async-done(((bf16[2048,1,1024]{2,0,1:T(8,128)(2,1)}), bf16[256,1,1024]{2,0,1:T(8,128)(2,1)}) %reduce-scatter.36.cloned.1.call-update) | async-done | bytes 524304 | tf_op jit(solution)/shard_map/reduce_scatter | solution.py:277
  (482 shorter events, 317.8 us)
Async XLA Ops:
  7.2 454.5 %copy-start = (bf16[1024,512]{1,0:T(8,128)(2,1)S(1)}, bf16[1024,512]{1,0:T(8,128)(2,1)}, u32[]{:S(2)}) copy-start(bf16[1024,512]{1,0:T(8,128)(2,1)} %param.28) | copy-start | bytes 3145732
  7.2 79.1 %all-gather.9.cloned.1.call-start = ((), (), s32[]{:S(2)}) async-start(), calls=%async_computation.15 | async-start | bytes 4718592 | tf_op jit(solution)/shard_map/all_gather | solution.py:98
  10.6 187.3 %reduce-scatter.22.cloned.1.call-start = ((), (), s32[]{:S(2)}) async-start(), calls=%async_computation.16 | async-start | bytes 4718592 | tf_op jit(solution)/shard_map/reduce_scatter | solution.py:143
  110.9 162.4 %all-gather.13.cloned.1.call-start = ((), (), s32[]{:S(2)}) async-start(), calls=%async_computation.19 | async-start | bytes 4718592 | tf_op jit(solution)/shard_map/all_gather | solution.py:98
  200.8 185.3 %reduce-scatter.26.cloned.1.call-start = ((), (), s32[]{:S(2)}) async-start(), calls=%async_computation.20 | async-start | bytes 4718592 | tf_op jit(solution)/shard_map/reduce_scatter | solution.py:143
  299.0 162.6 %all-gather.11.cloned.1.call-start = ((), (), s32[]{:S(2)}) async-start(), calls=%async_computation.17 | async-start | bytes 4718592 | tf_op jit(solution)/shard_map/all_gather | solution.py:155
  389.1 179.4 %reduce-scatter.24.cloned.1.call-start = ((), (), s32[]{:S(2)}) async-start(), calls=%async_computation.18 | async-start | bytes 4718592 | tf_op jit(solution)/shard_map/reduce_scatter | solution.py:161
  481.5 167.5 %all-gather.17.cloned.1.call-start = ((), (), s32[]{:S(2)}) async-start(), calls=%async_computation.23 | async-start | bytes 4718592 | tf_op jit(solution)/shard_map/all_gather | solution.py:183
  576.4 172.2 %reduce-scatter.30.cloned.1.call-start = ((), (), s32[]{:S(2)}) async-start(), calls=%async_computation.24 | async-start | bytes 4718592 | tf_op jit(solution)/shard_map/reduce_scatter | solution.py:195
  661.6 164.0 %all-gather.15.cloned.1.call-start = ((), (), s32[]{:S(2)}) async-start(), calls=%async_computation.21 | async-start | bytes 4718592 | tf_op jit(solution)/shard_map/all_gather | solution.py:155
  753.1 179.1 %reduce-scatter.28.cloned.1.call-start = ((), (), s32[]{:S(2)}) async-start(), calls=%async_computation.22 | async-start | bytes 4718592 | tf_op jit(solution)/shard_map/reduce_scatter | solution.py:161
  845.2 167.1 %all-gather.21.cloned.1.call-start = ((), (), s32[]{:S(2)}) async-start(), calls=%async_computation.27 | async-start | bytes 4718592 | tf_op jit(solution)/shard_map/all_gather | solution.py:183
  939.7 145.9 %all-gather.19.cloned.1.call-start = ((), (), s32[]{:S(2)}) async-start(), calls=%async_computation.25 | async-start | bytes 4718592 | tf_op jit(solution)/shard_map/all_gather | solution.py:208
  944.2 231.9 %reduce-scatter.34.cloned.1.call-start = ((), (), s32[]{:S(2)}) async-start(), calls=%async_computation.28 | async-start | bytes 4718592 | tf_op jit(solution)/shard_map/reduce_scatter | solution.py:195
  1025.1 241.8 %all-gather.23.cloned.1.call-start = ((), (), s32[]{:S(2)}) async-start(), calls=%async_computation.29 | async-start | bytes 4718592 | tf_op jit(solution)/shard_map/all_gather | solution.py:208
  1182.8 163.8 %reduce-scatter.32.cloned.1.call-start = ((), (), s32[]{:S(2)}) async-start(), calls=%async_computation.26 | async-start | bytes 4718592 | tf_op jit(solution)/shard_map/reduce_scatter | solution.py:277
  1246.9 121.0 %reduce-scatter.48.cloned.1.call-start = ((), (), s32[]{:S(2)}) async-start(), calls=%async_computation.36 | async-start | bytes 163840
  1248.4 146.7 %reduce-scatter.44.cloned.1.call-start = ((), (), s32[]{:S(2)}) async-start(), calls=%async_computation.34 | async-start | bytes 1310720 | tf_op jit(solution)/shard_map/reduce_scatter | solution.py:301
  1256.6 166.3 %reduce-scatter.42.cloned.1.call-start = ((), (), s32[]{:S(2)}) async-start(), calls=%async_computation.33 | async-start | bytes 1310720 | tf_op jit(solution)/shard_map/reduce_scatter | solution.py:301
  1264.9 296.2 %reduce-scatter.50.cloned.1.call-start = ((), (), s32[]{:S(2)}) async-start(), calls=%async_computation.37 | async-start | bytes 540672
  1266.9 312.3 %reduce-scatter.46.cloned.1.call-start = ((), (), s32[]{:S(2)}) async-start(), calls=%async_computation.35 | async-start | bytes 40960
  1323.8 278.5 %reduce-scatter.40.cloned.1.call-start = ((), (), s32[]{:S(2)}) async-start(), calls=%async_computation.32 | async-start | bytes 327680 | tf_op jit(solution)/shard_map/reduce_scatter | solution.py:301
  1330.8 297.2 %reduce-scatter.38.cloned.1.call-start = ((), (), s32[]{:S(2)}) async-start(), calls=%async_computation.31 | async-start | bytes 983040 | tf_op jit(solution)/shard_map/reduce_scatter | solution.py:301
  1338.7 381.4 %reduce-scatter.36.cloned.1.call-start = ((), (), s32[]{:S(2)}) async-start(), calls=%async_computation.30 | async-start | bytes 4718592 | tf_op jit(solution)/shard_map/reduce_scatter | solution.py:277
  (136 other events, 3120.9 us)
Sparse Core Ops, SparseCore 0:
  10.7 75.5 all-gather.8
  111.0 86.8 reduce-scatter.21
  200.9 72.4 all-gather.12
  299.2 86.8 reduce-scatter.25
  389.2 72.4 all-gather.10
  481.6 86.8 reduce-scatter.23
  576.5 72.4 all-gather.16
  661.8 86.8 reduce-scatter.29
  753.2 72.4 all-gather.14
  845.3 86.8 reduce-scatter.27
  939.8 72.4 all-gather.20
  1014.3 71.3 all-gather.18
  1089.2 86.8 reduce-scatter.33
  1182.9 72.4 all-gather.22
  1258.9 86.8 reduce-scatter.31
  1348.6 19.2 reduce-scatter.47
  1370.3 24.7 reduce-scatter.43
  1398.0 24.7 reduce-scatter.41
  1425.1 135.8 reduce-scatter.49
  1563.3 15.8 reduce-scatter.45
  1582.2 20.0 reduce-scatter.39
  1604.8 23.1 reduce-scatter.37
  1631.7 88.3 reduce-scatter.35
where the time goes:
time: 1740 us; the launch traced here: 1730 us
  waiting for transfers between devices  1360 us (78%)
  matrix products  224 us (13%)
  other arithmetic  89 us (5%)
  local copies, waits for them, and re-layouts  39.1 us (2%)
    reduce_scatter x2, waiting for transfers between devices, body(): lax.psum_scatter(jnp.einsum('sic,cd->sid', context, out_weight, preferred...  174 us
    unnamed x26, waiting for transfers between devices  174 us
    reduce_scatter x2, waiting for transfers between devices, body(): lax.psum_scatter(jnp.einsum('sif,df->sid', grad_pre, up_weight, preferred...  166 us
    reduce_scatter x2, waiting for transfers between devices, body(): lax.psum_scatter(jnp.einsum('sif,fd->sid', act_low, down_weight, preferre...  163 us
    all_gather x2, waiting for transfers between devices, body(): normed_all = lax.all_gather(normed_low, 'tensor', axis=0, tiled=True)  145 us
    all_gather x2, waiting for transfers between devices, body(): hidden_all = lax.all_gather(hidden_low, 'tensor', axis=0, tiled=True)  145 us
    all_gather x2, waiting for transfers between devices, body(): lax.all_gather(grad_sum.astype(jnp.bfloat16), 'tensor', axis=0, tiled=True)  140 us
    reduce_scatter x4, waiting for transfers between devices, body(): lax.psum_scatter(as_sent(totals), 'dp', scatter_dimension=1, tiled=True)  97.9 us
  transfers between devices with their start and end apart: 23, of which 21 were waited for; matrix products, arithmetic and copies ran while one was open for 11% of the time, Pallas kernels for 0%

commit v1 on v0

--- a/solution.py
+++ b/solution.py
@@ -95,7 +95,20 @@
         temb = jnp.where(late[:, None, None], embedded[None, :, 1], embedded[None, :, 0])
         hidden = tokens[index].astype(jnp.float32) + temb
         hidden_low = hidden.astype(jnp.bfloat16)
-        hidden_all = lax.all_gather(hidden_low, "tensor", axis=0, tiled=True)
+        arr_next = lax.axis_size("tensor")
+        tmp = lax.axis_index("tensor")
+        current_arr, mixed_arr = (arr_next, tmp)
+        hidden_all, block_out = (hidden_low, 1)
+        while block_out < current_arr:
+            ready = lax.ppermute(
+                hidden_all,
+                axis_name="tensor",
+                perm=[(dev_i, dev_i ^ block_out) for dev_i in range(current_arr)],
+            )
+            outcome_arr = jnp.concatenate([hidden_all, ready], axis=0)
+            n_now = jnp.concatenate([ready, hidden_all], axis=0)
+            hidden_all = jnp.where(mixed_arr & block_out == 0, outcome_arr, n_now)
+            block_out = 2 * block_out
         projected = jnp.einsum(
             "sid,kdc->ksic", hidden_all, qkv_weight, preferred_element_type=jnp.float32
         )

time: 1740 us -> 1860 us (1.069)
  waiting for transfers between devices: 1360 us -> 1450 us
    ppermute x0 -> x6, waiting for transfers between devices: none -> 237 us  [body(): lax.ppermute(hidden_all, axis_name='tensor', perm=[(dev_i, dev_i ^ block_...]
    all_gather x2 -> x0, waiting for transfers between devices: 145 us -> none  [body(): hidden_all = lax.all_gather(hidden_low, 'tensor', axis=0, tiled=True)]
    unnamed x26 -> x24, waiting for transfers between devices: 174 us -> 168 us
  transfers between devices with their start and end apart: 23 -> 27, of which waited for: 21 -> 25; matrix products, arithmetic and copies ran while one was open for 11% -> 11% of each run, Pallas kernels for 0% -> 0%
where the time goes in v1:
time: 1860 us
  waiting for transfers between devices  1450 us (78%)
  matrix products  230 us (12%)
  other arithmetic  103 us (6%)
  local copies, waits for them, and re-layouts  38.8 us (2%)
    ppermute x6, waiting for transfers between devices, body(): lax.ppermute(hidden_all, axis_name='tensor', perm=[(dev_i, dev_i ^ block_...  237 us
    reduce_scatter x2, waiting for transfers between devices, body(): lax.psum_scatter(jnp.einsum('sic,cd->sid', context, out_weight, preferred...  179 us
    unnamed x24, waiting for transfers between devices  168 us
    reduce_scatter x2, waiting for transfers between devices, body(): lax.psum_scatter(jnp.einsum('sif,df->sid', grad_pre, up_weight, preferred...  166 us
    reduce_scatter x2, waiting for transfers between devices, body(): lax.psum_scatter(jnp.einsum('sif,fd->sid', act_low, down_weight, preferre...  163 us
    all_gather x2, waiting for transfers between devices, body(): normed_all = lax.all_gather(normed_low, 'tensor', axis=0, tiled=True)  145 us
    all_gather x2, waiting for transfers between devices, body(): lax.all_gather(grad_sum.astype(jnp.bfloat16), 'tensor', axis=0, tiled=True)  140 us
    reduce_scatter x4, waiting for transfers between devices, body(): lax.psum_scatter(as_sent(totals), 'dp', scatter_dimension=1, tiled=True)  97.8 us
  transfers between devices with their start and end apart: 27, of which 25 were waited for; matrix products, arithmetic and copies ran while one was open for 11% of the time, Pallas kernels for 0%

profile of v1, /device:TPU:0, one launch (start us, length us, event | category | flops | bytes accessed | tf_op | source)
XLA Modules:
  0.0 1857.4 jit_solution(12006497996320003688)
XLA Ops:
  29.4 21.2 %collective-permute-done.1 = bf16[512,1,1024]{2,0,1:T(8,128)(2,1)} collective-permute-done((bf16[512,1,1024]{2,0,1:T(8,128)(2,1)}, bf16[512,1,1024]{2,0,1:T(8,128)(2,1)}, u32[]{:S(2)}, u32[]{:S(2)}) %collective-permute-start.1) | collective-permute-done | bytes 1048608 | tf_op jit(solution)/shard_map/ppermute | solution.py:103
  62.3 84.3 %collective-permute-done.2 = bf16[1024,1,1024]{2,0,1:T(8,128)(2,1)} collective-permute-done((bf16[1024,1,1024]{2,0,1:T(8,128)(2,1)}, bf16[1024,1,1024]{2,0,1:T(8,128)(2,1)}, u32[]{:S(2)}, u32[]{:S(2)}) %collective-permute-start.2) | collective-permute-done | bytes 2097184 | tf_op jit(solution)/shard_map/ppermute | solution.py:103
  176.7 89.2 %reduce-scatter.22.cloned.1.call-done = bf16[256,1,1024]{2,0,1:T(8,128)(2,1)} async-done(((bf16[2048,1,1024]{2,0,1:T(8,128)(2,1)}), bf16[256,1,1024]{2,0,1:T(8,128)(2,1)}) %reduce-scatter.22.cloned.1.call-update) | async-done | bytes 524304 | tf_op jit(solution)/shard_map/reduce_scatter | solution.py:156
  284.0 21.5 %collective-permute-done.4 = bf16[512,1,1024]{2,0,1:T(8,128)(2,1)S(1)} collective-permute-done((bf16[512,1,1024]{2,0,1:T(8,128)(2,1)S(1)}, bf16[512,1,1024]{2,0,1:T(8,128)(2,1)S(1)}, u32[]{:S(2)}, u32[]{:S(2)}) %collective-permute-start.4) | collective-permute-done | bytes 1048608 | tf_op jit(solution)/shard_map/ppermute | solution.py:103
  310.3 87.8 %collective-permute-done.5 = bf16[1024,1,1024]{2,0,1:T(8,128)(2,1)S(1)} collective-permute-done((bf16[1024,1,1024]{2,0,1:T(8,128)(2,1)S(1)}, bf16[1024,1,1024]{2,0,1:T(8,128)(2,1)S(1)}, u32[]{:S(2)}, u32[]{:S(2)}) %collective-permute-start.5) | collective-permute-done | bytes 2097184 | tf_op jit(solution)/shard_map/ppermute | solution.py:103
  421.8 89.4 %reduce-scatter.26.cloned.1.call-done = bf16[256,1,1024]{2,0,1:T(8,128)(2,1)} async-done(((bf16[2048,1,1024]{2,0,1:T(8,128)(2,1)}), bf16[256,1,1024]{2,0,1:T(8,128)(2,1)}) %reduce-scatter.26.cloned.1.call-update) | async-done | bytes 524304 | tf_op jit(solution)/shard_map/reduce_scatter | solution.py:156
  514.3 72.5 %all-gather.7.cloned.1.call-done = bf16[2048,1,1024]{2,0,1:T(8,128)(2,1)} async-done(((bf16[256,1,1024]{2,0,1:T(8,128)(2,1)}), bf16[2048,1,1024]{2,0,1:T(8,128)(2,1)}) %all-gather.7.cloned.1.call-update) | async-done | bytes 4194320 | tf_op jit(solution)/shard_map/all_gather | solution.py:168
  616.8 77.0 %reduce-scatter.24.cloned.1.call-done = bf16[256,1,1024]{2,0,1:T(8,128)(2,1)} async-done(((bf16[2048,1,1024]{2,0,1:T(8,128)(2,1)}), bf16[256,1,1024]{2,0,1:T(8,128)(2,1)}) %reduce-scatter.24.cloned.1.call-update) | async-done | bytes 524304 | tf_op jit(solution)/shard_map/reduce_scatter | solution.py:174
  701.8 72.5 %all-gather.11.cloned.1.call-done = bf16[2048,1,1024]{2,0,1:T(8,128)(2,1)} async-done(((bf16[256,1,1024]{2,0,1:T(8,128)(2,1)}), bf16[2048,1,1024]{2,0,1:T(8,128)(2,1)}) %all-gather.11.cloned.1.call-update) | async-done | bytes 4194320 | tf_op jit(solution)/shard_map/all_gather | solution.py:196
  787.2 86.8 %reduce-scatter.30.cloned.1.call-done = bf16[256,1,1024]{2,0,1:T(8,128)(2,1)} async-done(((bf16[2048,1,1024]{2,0,1:T(8,128)(2,1)}), bf16[256,1,1024]{2,0,1:T(8,128)(2,1)}) %reduce-scatter.30.cloned.1.call-update) | async-done | bytes 524304 | tf_op jit(solution)/shard_map/reduce_scatter | solution.py:208
  878.4 72.5 %all-gather.9.cloned.1.call-done = bf16[2048,1,1024]{2,0,1:T(8,128)(2,1)} async-done(((bf16[256,1,1024]{2,0,1:T(8,128)(2,1)}), bf16[2048,1,1024]{2,0,1:T(8,128)(2,1)}) %all-gather.9.cloned.1.call-update) | async-done | bytes 4194320 | tf_op jit(solution)/shard_map/all_gather | solution.py:168
  971.1 86.3 %reduce-scatter.28.cloned.1.call-done = bf16[256,1,1024]{2,0,1:T(8,128)(2,1)} async-done(((bf16[2048,1,1024]{2,0,1:T(8,128)(2,1)}), bf16[256,1,1024]{2,0,1:T(8,128)(2,1)}) %reduce-scatter.28.cloned.1.call-update) | async-done | bytes 524304 | tf_op jit(solution)/shard_map/reduce_scatter | solution.py:174
  1069.7 67.8 %all-gather.15.cloned.1.call-done = bf16[2048,1,1024]{2,0,1:T(8,128)(2,1)} async-done(((bf16[256,1,1024]{2,0,1:T(8,128)(2,1)}), bf16[2048,1,1024]{2,0,1:T(8,128)(2,1)}) %all-gather.15.cloned.1.call-update) | async-done | bytes 4194320 | tf_op jit(solution)/shard_map/all_gather | solution.py:196
  1150.3 60.6 %all-gather.13.cloned.1.call-done = bf16[2048,1,1024]{2,0,1:T(8,128)(2,1)} async-done(((bf16[256,1,1024]{2,0,1:T(8,128)(2,1)}), bf16[2048,1,1024]{2,0,1:T(8,128)(2,1)}) %all-gather.13.cloned.1.call-update) | async-done | bytes 4194320 | tf_op jit(solution)/shard_map/all_gather | solution.py:221
  1221.9 79.5 %reduce-scatter.34.cloned.1.call-done = bf16[256,1,1024]{2,0,1:T(8,128)(2,1)} async-done(((bf16[2048,1,1024]{2,0,1:T(8,128)(2,1)}), bf16[256,1,1024]{2,0,1:T(8,128)(2,1)}) %reduce-scatter.34.cloned.1.call-update) | async-done | bytes 524304 | tf_op jit(solution)/shard_map/reduce_scatter | solution.py:208
  1317.9 15.2 multiply_reduce_fusion.1
  1478.5 14.8 reduce-scatter.48.cloned.1.call-done
  1494.6 25.8 %reduce-scatter.44.cloned.1.call-done = bf16[512,256]{1,0:T(8,128)(2,1)} async-done(((bf16[512,1024]{1,0:T(8,128)(2,1)}), bf16[512,256]{1,0:T(8,128)(2,1)}) %reduce-scatter.44.cloned.1.call-update) | async-done | bytes 262160 | tf_op jit(solution)/shard_map/reduce_scatter | solution.py:314
  1522.2 25.4 %reduce-scatter.42.cloned.1.call-done = bf16[1,256,512]{2,1,0:T(8,128)(2,1)} async-done(((bf16[1,1024,512]{2,1,0:T(8,128)(2,1)}), bf16[1,256,512]{2,1,0:T(8,128)(2,1)}) %reduce-scatter.42.cloned.1.call-update) | async-done | bytes 262160 | tf_op jit(solution)/shard_map/reduce_scatter | solution.py:314
  1549.5 136.1 %reduce-scatter.50.cloned.1.call-done = f32[32,6]{1,0:T(8,128)} async-done(((f32[1024,6]{1,0:T(8,128)}), f32[32,6]{1,0:T(8,128)}) %reduce-scatter.50.cloned.1.call-update) | async-done | bytes 784
  1687.0 16.8 reduce-scatter.46.cloned.1.call-done
  1705.1 21.8 %reduce-scatter.40.cloned.1.call-done = bf16[128,256]{1,0:T(8,128)(2,1)} async-done(((bf16[128,1024]{1,0:T(8,128)(2,1)}), bf16[128,256]{1,0:T(8,128)(2,1)}) %reduce-scatter.40.cloned.1.call-update) | async-done | bytes 65552 | tf_op jit(solution)/shard_map/reduce_scatter | solution.py:314
  1728.4 24.7 %reduce-scatter.38.cloned.1.call-done = bf16[3,256,128]{1,2,0:T(8,128)(2,1)} async-done(((bf16[3,1024,128]{1,2,0:T(8,128)(2,1)}), bf16[3,256,128]{1,2,0:T(8,128)(2,1)}) %reduce-scatter.38.cloned.1.call-update) | async-done | bytes 196624 | tf_op jit(solution)/shard_map/reduce_scatter | solution.py:314
  1754.9 90.2 %reduce-scatter.36.cloned.1.call-done = bf16[256,1,1024]{2,0,1:T(8,128)(2,1)} async-done(((bf16[2048,1,1024]{2,0,1:T(8,128)(2,1)}), bf16[256,1,1024]{2,0,1:T(8,128)(2,1)}) %reduce-scatter.36.cloned.1.call-update) | async-done | bytes 524304 | tf_op jit(solution)/shard_map/reduce_scatter | solution.py:290
  (509 shorter events, 400.8 us)
Async XLA Ops:
  7.2 258.7 %reduce-scatter.22.cloned.1.call-start = ((), (), s32[]{:S(2)}) async-start(), calls=%async_computation.15 | async-start | bytes 4718592 | tf_op jit(solution)/shard_map/reduce_scatter | solution.py:156
  26.0 24.6 %collective-permute-start.1 = (bf16[512,1,1024]{2,0,1:T(8,128)(2,1)}, bf16[512,1,1024]{2,0,1:T(8,128)(2,1)}, u32[]{:S(2)}, u32[]{:S(2)}) collective-permute-start(bf16[512,1,1024]{2,0,1:T(8,128)(2,1)} %maximum_select_fusion.7), channel_id=1, source_target_pairs={{0,2},{1,3},{2,0},{3,1},{4,6},{5,7},{6,4},{7,5},{8,10},{9,11},{10,... | collective-permute-start | bytes 3145736 | tf_op jit(solution)/shard_map/ppermute | solution.py:103
  54.5 92.1 %collective-permute-start.2 = (bf16[1024,1,1024]{2,0,1:T(8,128)(2,1)}, bf16[1024,1,1024]{2,0,1:T(8,128)(2,1)}, u32[]{:S(2)}, u32[]{:S(2)}) collective-permute-start(bf16[1024,1,1024]{2,0,1:T(8,128)(2,1)} %maximum_select_fusion.3), channel_id=1, source_target_pairs={{0,4},{1,5},{2,6},{3,7},{4,0},{5,1},{6,2},{7,3},{8,12},{9,13},{10,... | collective-permute-start | bytes 6291464 | tf_op jit(solution)/shard_map/ppermute | solution.py:103
  176.6 334.6 %reduce-scatter.26.cloned.1.call-start = ((), (), s32[]{:S(2)}) async-start(), calls=%async_computation.18 | async-start | bytes 4718592 | tf_op jit(solution)/shard_map/reduce_scatter | solution.py:156
  306.5 91.6 %collective-permute-start.5 = (bf16[1024,1,1024]{2,0,1:T(8,128)(2,1)S(1)}, bf16[1024,1,1024]{2,0,1:T(8,128)(2,1)S(1)}, u32[]{:S(2)}, u32[]{:S(2)}) collective-permute-start(bf16[1024,1,1024]{2,0,1:T(8,128)(2,1)S(1)} %maximum_select_fusion.5), channel_id=1, source_target_pairs={{0,4},{1,5},{2,6},{3,7},{4,0},{5,1},{6,2},{7,3},{8,12},{9,13},{10,... | collective-permute-start | bytes 6291464 | tf_op jit(solution)/shard_map/ppermute | solution.py:103
  421.7 165.1 %all-gather.7.cloned.1.call-start = ((), (), s32[]{:S(2)}) async-start(), calls=%async_computation.16 | async-start | bytes 4718592 | tf_op jit(solution)/shard_map/all_gather | solution.py:168
  514.2 179.6 %reduce-scatter.24.cloned.1.call-start = ((), (), s32[]{:S(2)}) async-start(), calls=%async_computation.17 | async-start | bytes 4718592 | tf_op jit(solution)/shard_map/reduce_scatter | solution.py:174
  606.8 167.5 %all-gather.11.cloned.1.call-start = ((), (), s32[]{:S(2)}) async-start(), calls=%async_computation.21 | async-start | bytes 4718592 | tf_op jit(solution)/shard_map/all_gather | solution.py:196
  701.7 172.2 %reduce-scatter.30.cloned.1.call-start = ((), (), s32[]{:S(2)}) async-start(), calls=%async_computation.22 | async-start | bytes 4718592 | tf_op jit(solution)/shard_map/reduce_scatter | solution.py:208
  786.9 164.0 %all-gather.9.cloned.1.call-start = ((), (), s32[]{:S(2)}) async-start(), calls=%async_computation.19 | async-start | bytes 4718592 | tf_op jit(solution)/shard_map/all_gather | solution.py:168
  878.4 179.0 %reduce-scatter.28.cloned.1.call-start = ((), (), s32[]{:S(2)}) async-start(), calls=%async_computation.20 | async-start | bytes 4718592 | tf_op jit(solution)/shard_map/reduce_scatter | solution.py:174
  970.4 167.1 %all-gather.15.cloned.1.call-start = ((), (), s32[]{:S(2)}) async-start(), calls=%async_computation.25 | async-start | bytes 4718592 | tf_op jit(solution)/shard_map/all_gather | solution.py:196
  1065.0 145.9 %all-gather.13.cloned.1.call-start = ((), (), s32[]{:S(2)}) async-start(), calls=%async_computation.23 | async-start | bytes 4718592 | tf_op jit(solution)/shard_map/all_gather | solution.py:221
  1069.5 231.9 %reduce-scatter.34.cloned.1.call-start = ((), (), s32[]{:S(2)}) async-start(), calls=%async_computation.26 | async-start | bytes 4718592 | tf_op jit(solution)/shard_map/reduce_scatter | solution.py:208
  1150.2 243.8 %all-gather.17.cloned.1.call-start = ((), (), s32[]{:S(2)}) async-start(), calls=%async_computation.27 | async-start | bytes 4718592 | tf_op jit(solution)/shard_map/all_gather | solution.py:221
  1308.1 169.3 %reduce-scatter.32.cloned.1.call-start = ((), (), s32[]{:S(2)}) async-start(), calls=%async_computation.24 | async-start | bytes 4718592 | tf_op jit(solution)/shard_map/reduce_scatter | solution.py:290
  1373.5 119.8 %reduce-scatter.48.cloned.1.call-start = ((), (), s32[]{:S(2)}) async-start(), calls=%async_computation.34 | async-start | bytes 163840
  1375.0 145.5 %reduce-scatter.44.cloned.1.call-start = ((), (), s32[]{:S(2)}) async-start(), calls=%async_computation.32 | async-start | bytes 1310720 | tf_op jit(solution)/shard_map/reduce_scatter | solution.py:314
  1383.2 164.5 %reduce-scatter.42.cloned.1.call-start = ((), (), s32[]{:S(2)}) async-start(), calls=%async_computation.31 | async-start | bytes 1310720 | tf_op jit(solution)/shard_map/reduce_scatter | solution.py:314
  1391.5 294.1 %reduce-scatter.50.cloned.1.call-start = ((), (), s32[]{:S(2)}) async-start(), calls=%async_computation.35 | async-start | bytes 540672
  1394.0 309.7 %reduce-scatter.46.cloned.1.call-start = ((), (), s32[]{:S(2)}) async-start(), calls=%async_computation.33 | async-start | bytes 40960
  1450.9 276.0 %reduce-scatter.40.cloned.1.call-start = ((), (), s32[]{:S(2)}) async-start(), calls=%async_computation.30 | async-start | bytes 327680 | tf_op jit(solution)/shard_map/reduce_scatter | solution.py:314
  1458.3 294.8 %reduce-scatter.38.cloned.1.call-start = ((), (), s32[]{:S(2)}) async-start(), calls=%async_computation.29 | async-start | bytes 983040 | tf_op jit(solution)/shard_map/reduce_scatter | solution.py:314
  1469.2 375.9 %reduce-scatter.36.cloned.1.call-start = ((), (), s32[]{:S(2)}) async-start(), calls=%async_computation.28 | async-start | bytes 4718592 | tf_op jit(solution)/shard_map/reduce_scatter | solution.py:290
  (146 other events, 3926.6 us)
Sparse Core Ops, SparseCore 0:
  176.7 89.1 reduce-scatter.21
  421.8 89.3 reduce-scatter.25
  514.3 72.4 all-gather.6
  606.9 86.8 reduce-scatter.23
  701.8 72.4 all-gather.10
  787.1 86.8 reduce-scatter.29
  878.5 72.4 all-gather.8
  970.6 86.8 reduce-scatter.27
  1065.1 72.4 all-gather.14
  1139.5 71.3 all-gather.12
  1214.5 86.8 reduce-scatter.33
  1308.2 72.4 all-gather.16
  1384.3 86.8 reduce-scatter.31
  1474.0 19.2 reduce-scatter.47
  1495.6 24.7 reduce-scatter.43
  1522.8 24.7 reduce-scatter.41
  1549.8 135.8 reduce-scatter.49
  1687.9 15.8 reduce-scatter.45
  1706.8 20.0 reduce-scatter.39
  1729.8 23.2 reduce-scatter.37
  1756.7 88.3 reduce-scatter.35
